TPU v7x, 128 devices: a whole 4x4x4 slice. The times are simulated.
128 devices in a mesh: wide: 32 (over x, y, z_lo), narrow: 4 (over z_hi, core).
Axes of the slice: x: 4, y: 4, z: 4 (z_hi: 2, z_lo: 2; z = z_hi * 2 + z_lo), core: 2. Of those that a mesh axis runs over, the one named last changes fastest.
Arguments:
- mlp_input: bfloat16 [768, 5120], P('wide', 'narrow'), may hold values from -6 to 6
- grad_rows: bfloat16 [768, 5120], P('wide', 'narrow'), may hold values from -18 to 18
- enc_weight: bfloat16 [5120, 65536], P('narrow', 'wide'), may hold values from -0.078125 to 0.078125
- enc_bias: float32 [65536], P('wide'), may hold values from -3 to 3
- dec_weight: bfloat16 [65536, 5120], P('wide', 'narrow'), may hold values from -0.0234375 to 0.0234375
- dec_bias: float32 [5120], P('narrow'), may hold values from -3 to 3
Outputs:
- recon: bfloat16 [768, 5120], P('wide', 'narrow')
- attribution: bfloat16 [768, 65536], P(None, 'wide')
All inputs are finite; a program needn't handle non-finite values.
Results may differ from a plain program's by a relative error of at most 0.023.
Values may be sent and summed in bfloat16 or wider, within the bound.
No kernel may reach another device: no remote copies, remote signals or barrier semaphores. Data moves between devices by JAX's collectives and lax.ppermute only.
A program may use at most 64 MiB of HBM per device.

v0:
```python
import jax
import jax.numpy as jnp
from jax import lax
from jax.sharding import PartitionSpec as P


def local(mlp_input, grad_rows, enc_weight, enc_bias, dec_weight, dec_bias):
    enc_terms = jnp.dot(
        lax.all_gather(mlp_input, "wide", axis=0, tiled=True),
        enc_weight,
        preferred_element_type=jnp.float32,
    )
    grad_terms = lax.dot_general(
        lax.all_gather(grad_rows, "wide", axis=0, tiled=True),
        dec_weight,
        (((1,), (1,)), ((), ())),
        preferred_element_type=jnp.float32,
    )
    pre, grad_proj = (
        lax.psum(enc_terms.astype(jnp.bfloat16), "narrow").astype(jnp.float32),
        lax.psum(grad_terms.astype(jnp.bfloat16), "narrow").astype(jnp.float32),
    )
    latents = jnp.maximum(pre + enc_bias[None, :], 0.0).astype(jnp.bfloat16)
    attribution = (latents.astype(jnp.float32) * grad_proj).astype(jnp.bfloat16)
    recon_sum = lax.psum_scatter(
        jnp.dot(latents, dec_weight, preferred_element_type=jnp.float32).astype(jnp.bfloat16),
        "wide",
        scatter_dimension=0,
        tiled=True,
    ).astype(jnp.float32)
    recon = (recon_sum + dec_bias[None, :]).astype(jnp.bfloat16)
    return (recon, attribution)


def solution(mesh):
    placed = (
        P("wide", "narrow"),
        P("wide", "narrow"),
        P("narrow", "wide"),
        P("wide"),
        P("wide", "narrow"),
        P("narrow"),
    )
    return jax.shard_map(
        local,
        mesh=mesh,
        in_specs=placed,
        out_specs=(P("wide", "narrow"), P(None, "wide")),
        check_vma=False,
    )
```

profile of v0, /device:TPU:0, one launch (start us, length us, event | category | flops | bytes accessed | tf_op | source)
XLA Modules:
  0.0 636.6 jit_solution(16167423434379626418)
XLA Ops:
  7.2 0.0 all-gather.5.cloned.1.call-start
  7.2 0.7 all-gather.5.cloned.1.call-update
  7.9 0.0 all-gather.3.cloned.1.call-start
  7.9 0.7 all-gather.3.cloned.1.call-update
  8.6 0.0 all-reduce.3.cloned.1.call-start
  8.7 155.7 %all-gather.5.cloned.1.call-done = bf16[768,1280]{1,0:T(8,128)(2,1)} async-done(((bf16[24,1280]{1,0:T(8,128)(2,1)}), bf16[768,1280]{1,0:T(8,128)(2,1)}) %all-gather.5.cloned.1.call-update) | async-done | bytes 1966096 | tf_op jit(solution)/shard_map/all_gather | solution.py:14
  164.4 9.1 %convolution_convert_fusion = bf16[768,2048]{1,0:T(8,128)(2,1)} fusion(bf16[768,1280]{1,0:T(8,128)(2,1)} %all-gather.5.cloned.1.call-done, bf16[2048,1280]{1,0:T(8,128)(2,1)} %param.10), kind=kOutput, calls=%fused_computation.2 | convolution fusion | flops 4028104704 | bytes 10354688 | tf_op jit(solution)/shard_map/dot_general | solution.py:13
  173.4 145.1 %all-gather.3.cloned.1.call-done = bf16[768,1280]{1,0:T(8,128)(2,1)} async-done(((bf16[24,1280]{1,0:T(8,128)(2,1)}), bf16[768,1280]{1,0:T(8,128)(2,1)}) %all-gather.3.cloned.1.call-update) | async-done | bytes 1966096 | tf_op jit(solution)/shard_map/all_gather | solution.py:9
  318.5 9.0 %convolution_convert_fusion.2 = bf16[768,2048]{1,0:T(8,128)(2,1)} fusion(bf16[768,1280]{1,0:T(8,128)(2,1)} %all-gather.3.cloned.1.call-done, bf16[1280,2048]{1,0:T(8,128)(2,1)} %param.8), kind=kOutput, calls=%fused_computation.4 | convolution fusion | flops 4028104704 | bytes 10354688 | tf_op jit(solution)/shard_map/dot_general | solution.py:8
  327.5 0.0 copy-start.2
  327.5 0.0 all-reduce.3.cloned.1.call-update
  327.5 0.0 reduce-scatter.2.cloned.1.call-start
  327.6 127.1 %all-reduce.3.cloned.1.call-done = (bf16[768,2048]{1,0:T(8,128)(2,1)}, bf16[768,2048]{1,0:T(8,128)(2,1)}) async-done(((bf16[768,2048]{1,0:T(8,128)(2,1)}, bf16[768,2048]{1,0:T(8,128)(2,1)}), (bf16[768,2048]{1,0:T(8,128)(2,1)}, bf16[768,2048]{1,0:T(8,128)(2,1)})) %all-reduce.3.cloned.1.call-update) | async-done | bytes 6291472 | tf_op jit(solution)/shard_map/psum | solution.py:20
  454.7 0.0 copy-done.2
  454.7 0.0 copy-start
  454.7 9.1 %convolution_convert_fusion.1 = bf16[768,1280]{1,0:T(8,128)(2,1)} fusion(bf16[2048,1280]{1,0:T(8,128)(2,1)} %param.10, bf16[768,2048]{1,0:T(8,128)(2,1)} %get-tuple-element.2, f32[2048]{0:T(1024)S(1)} %copy-done.2), kind=kOutput, calls=%fused_computation.3 | convolution fusion | flops 4033806336 | bytes 10362880 | tf_op jit(solution)/shard_map/dot_general | solution.py:26
  463.8 0.0 copy-start.1
  463.8 0.0 reduce-scatter.2.cloned.1.call-update
  463.8 0.0 copy-done
  463.8 5.0 multiply_convert_fusion
  468.9 159.7 %reduce-scatter.2.cloned.1.call-done = bf16[24,1280]{1,0:T(8,128)(2,1)} async-done(((bf16[768,1280]{1,0:T(8,128)(2,1)}), bf16[24,1280]{1,0:T(8,128)(2,1)}) %reduce-scatter.2.cloned.1.call-update) | async-done | bytes 61456 | tf_op jit(solution)/shard_map/reduce_scatter | solution.py:25
  628.6 0.0 copy-done.1
  628.6 1.5 add_convert_fusion
Async XLA Ops:
  7.2 157.2 %all-gather.5.cloned.1.call-start = ((), (), s32[]{:S(2)}) async-start(), calls=%async_computation.3 | async-start | bytes 2027520 | tf_op jit(solution)/shard_map/all_gather | solution.py:14
  7.9 310.6 %all-gather.3.cloned.1.call-start = ((), (), s32[]{:S(2)}) async-start(), calls=%async_computation.1 | async-start | bytes 2027520 | tf_op jit(solution)/shard_map/all_gather | solution.py:9
  8.6 446.0 %all-reduce.3.cloned.1.call-start = ((), (), s32[]{:S(2)}) async-start(), calls=%async_computation.4 | async-start | bytes 12582912 | tf_op jit(solution)/shard_map/psum | solution.py:20
  327.5 127.2 %copy-start.2 = (f32[2048]{0:T(1024)S(1)}, f32[2048]{0:T(1024)}, u32[]{:S(2)}) copy-start(f32[2048]{0:T(1024)} %param.9) | copy-start | bytes 24580
  327.5 301.0 %reduce-scatter.2.cloned.1.call-start = ((), (), s32[]{:S(2)}) async-start(), calls=%async_computation.2 | async-start | bytes 2027520 | tf_op jit(solution)/shard_map/reduce_scatter | solution.py:25
  454.7 9.1 %copy-start = (bf16[768,2048]{1,0:T(8,128)(2,1)S(1)}, bf16[768,2048]{1,0:T(8,128)(2,1)}, u32[]{:S(2)}) copy-start(bf16[768,2048]{1,0:T(8,128)(2,1)} %get-tuple-element.2) | copy-start | bytes 9437188
  463.8 164.7 %copy-start.1 = (f32[1280]{0:T(1024)S(1)}, f32[1280]{0:T(1024)}, u32[]{:S(2)}) copy-start(f32[1280]{0:T(1024)} %param.11) | copy-start | bytes 15364
Sparse Core Ops, SparseCore 0:
  9.6 154.7 all-gather.4
  166.0 152.4 all-gather.2
  327.7 126.9 all-reduce.2
  464.0 164.5 reduce-scatter.1
where the time goes:
time: 637 us
  waiting for transfers between devices  589 us (92%)
  matrix products  27.1 us (4%)
  between operations  13.8 us (2%)
  other arithmetic  6.51 us (1%)
    reduce_scatter x1, waiting for transfers between devices, local(): lax.psum_scatter(jnp.dot(latents, dec_weight, preferred_element_type=jnp....  160 us
    all_gather x1, waiting for transfers between devices, local(): lax.all_gather(grad_rows, 'wide', axis=0, tiled=True)  156 us
    all_gather x1, waiting for transfers between devices, local(): lax.all_gather(mlp_input, 'wide', axis=0, tiled=True)  145 us
    psum x1, waiting for transfers between devices, local(): lax.psum(enc_terms.astype(jnp.bfloat16), 'narrow').astype(jnp.float32)  127 us
  transfers between devices with their start and end apart: 4, of which 4 were waited for; matrix products, arithmetic and copies ran while one was open for 2% of the time, Pallas kernels for 0%

commit v1 on v0

--- a/solution.py
+++ b/solution.py
@@ -1,15 +1,22 @@
+import functools
 import jax
 import jax.numpy as jnp
 from jax import lax
 from jax.sharding import PartitionSpec as P
+from jax.lax import all_to_all, axis_size
+
+
+def advance_sections(row_data, axis_name):
+    prior = tuple((row_data for _ in range(axis_size(axis_name))))
+    aux = all_to_all(jnp.stack(prior), axis_name, 0, 0)
+    return jnp.concatenate(aux, 0)
+
+
+lead_rows = functools.partial(advance_sections, axis_name="wide")
 
 
 def local(mlp_input, grad_rows, enc_weight, enc_bias, dec_weight, dec_bias):
-    enc_terms = jnp.dot(
-        lax.all_gather(mlp_input, "wide", axis=0, tiled=True),
-        enc_weight,
-        preferred_element_type=jnp.float32,
-    )
+    enc_terms = jnp.dot(lead_rows(mlp_input), enc_weight, preferred_element_type=jnp.float32)
     grad_terms = lax.dot_general(
         lax.all_gather(grad_rows, "wide", axis=0, tiled=True),
         dec_weight,

time: 637 us -> 498 us (0.78)
  waiting for transfers between devices: 589 us -> 416 us
  blocking collectives: 0 us -> 36.1 us
    all_gather x1 -> x0, waiting for transfers between devices: 145 us -> none  [local(): lax.all_gather(mlp_input, 'wide', axis=0, tiled=True)]
    all_to_all x0 -> x1, blocking collectives: none -> 36.1 us  [advance_sections(): aux = all_to_all(jnp.stack(prior), axis_name, 0, 0)]
    all_gather x1, waiting for transfers between devices: 156 us -> 130 us  [local(): lax.all_gather(grad_rows, 'wide', axis=0, tiled=True)]
  transfers between devices with their start and end apart: 4 -> 3, of which waited for: 4 -> 3; matrix products, arithmetic and copies ran while one was open for 2% -> 2% of each run, Pallas kernels for 0% -> 0%
where the time goes in v1:
time: 498 us
  waiting for transfers between devices  416 us (84%)
  blocking collectives  36.1 us (7%)
  matrix products  23.7 us (5%)
  between operations  13.8 us (3%)
  other arithmetic  6.6 us (1%)
    reduce_scatter x1, waiting for transfers between devices, local(): lax.psum_scatter(jnp.dot(latents, dec_weight, preferred_element_type=jnp....  159 us
    all_gather x1, waiting for transfers between devices, local(): lax.all_gather(grad_rows, 'wide', axis=0, tiled=True)  130 us
    psum x1, waiting for transfers between devices, local(): lax.psum(enc_terms.astype(jnp.bfloat16), 'narrow').astype(jnp.float32)  126 us
    all_to_all x1, blocking collectives, advance_sections(): aux = all_to_all(jnp.stack(prior), axis_name, 0, 0)  36.1 us
  transfers between devices with their start and end apart: 3, of which 3 were waited for; matrix products, arithmetic and copies ran while one was open for 2% of the time, Pallas kernels for 0%

profile of v1, /device:TPU:0, one launch (start us, length us, event | category | flops | bytes accessed | tf_op | source)
XLA Modules:
  0.0 497.7 jit_solution(10654329607562960262)
XLA Ops:
  7.2 0.0 all-gather.2.cloned.1.call-start
  7.2 0.7 all-gather.2.cloned.1.call-update
  7.9 0.0 all-reduce.3.cloned.1.call-start
  7.9 0.0 copy-start.3
  8.0 1.1 stack.2
  9.1 36.1 %all_to_all.5 = bf16[32,24,1280]{2,1,0:T(8,128)(2,1)S(1)} all-to-all(bf16[32,24,1280]{2,1,0:T(8,128)(2,1)S(1)} %stack.2), channel_id=1, replica_groups=mesh['wide'=32,'narrow'=4] {'wide'}, dimensions={0} | all-to-all | bytes 3932160 | tf_op jit(solution)/shard_map/all_to_all | solution.py:11
  45.1 0.0 copy-done.3
  45.1 5.5 %convolution_convert_fusion.2 = bf16[768,2048]{1,0:T(8,128)(2,1)} fusion(bf16[768,1280]{1,0:T(8,128)(2,1)S(1)} %bitcast.6, bf16[1280,2048]{1,0:T(8,128)(2,1)S(1)} %copy-done.3), kind=kOutput, calls=%fused_computation.4 | convolution fusion | flops 4028104704 | bytes 10354688 | tf_op jit(solution)/shard_map/dot_general | solution.py:19
  50.7 130.1 %all-gather.2.cloned.1.call-done = bf16[768,1280]{1,0:T(8,128)(2,1)} async-done(((bf16[24,1280]{1,0:T(8,128)(2,1)}), bf16[768,1280]{1,0:T(8,128)(2,1)}) %all-gather.2.cloned.1.call-update) | async-done | bytes 1966096 | tf_op jit(solution)/shard_map/all_gather | solution.py:21
  180.8 9.0 %convolution_convert_fusion = bf16[768,2048]{1,0:T(8,128)(2,1)} fusion(bf16[768,1280]{1,0:T(8,128)(2,1)} %all-gather.2.cloned.1.call-done, bf16[2048,1280]{1,0:T(8,128)(2,1)} %param.10), kind=kOutput, calls=%fused_computation.2 | convolution fusion | flops 4028104704 | bytes 10354688 | tf_op jit(solution)/shard_map/dot_general | solution.py:20
  189.8 0.0 copy-start.2
  189.8 0.0 all-reduce.3.cloned.1.call-update
  189.8 0.0 reduce-scatter.2.cloned.1.call-start
  189.9 126.3 %all-reduce.3.cloned.1.call-done = (bf16[768,2048]{1,0:T(8,128)(2,1)}, bf16[768,2048]{1,0:T(8,128)(2,1)}) async-done(((bf16[768,2048]{1,0:T(8,128)(2,1)}, bf16[768,2048]{1,0:T(8,128)(2,1)}), (bf16[768,2048]{1,0:T(8,128)(2,1)}, bf16[768,2048]{1,0:T(8,128)(2,1)})) %all-reduce.3.cloned.1.call-update) | async-done | bytes 6291472 | tf_op jit(solution)/shard_map/psum | solution.py:27
  316.2 0.0 copy-done.2
  316.2 0.0 copy-start
  316.2 9.1 %convolution_convert_fusion.1 = bf16[768,1280]{1,0:T(8,128)(2,1)} fusion(bf16[2048,1280]{1,0:T(8,128)(2,1)} %param.10, bf16[768,2048]{1,0:T(8,128)(2,1)} %get-tuple-element.2, f32[2048]{0:T(1024)S(1)} %copy-done.2), kind=kOutput, calls=%fused_computation.3 | convolution fusion | flops 4033806336 | bytes 10362880 | tf_op jit(solution)/shard_map/dot_general | solution.py:33
  325.3 0.0 reduce-scatter.2.cloned.1.call-update
  325.4 0.0 copy-done
  325.4 0.0 copy-start.1
  325.4 5.1 %multiply_convert_fusion = bf16[768,2048]{1,0:T(8,128)(2,1)} fusion(bf16[768,2048]{1,0:T(8,128)(2,1)} %get-tuple-element.3, f32[2048]{0:T(1024)S(1)} %copy-done.2, bf16[768,2048]{1,0:T(8,128)(2,1)S(1)} %copy-done), kind=kLoop, calls=%fused_computation | loop fusion | flops 12582912 | bytes 9445376 | tf_op jit(solution)/shard_map/convert_element_type | solution.py:31
  330.5 159.2 %reduce-scatter.2.cloned.1.call-done = bf16[24,1280]{1,0:T(8,128)(2,1)} async-done(((bf16[768,1280]{1,0:T(8,128)(2,1)}), bf16[24,1280]{1,0:T(8,128)(2,1)}) %reduce-scatter.2.cloned.1.call-update) | async-done | bytes 61456 | tf_op jit(solution)/shard_map/reduce_scatter | solution.py:32
  489.7 0.0 copy-done.1
  489.7 1.5 add_convert_fusion
Async XLA Ops:
  7.2 173.6 %all-gather.2.cloned.1.call-start = ((), (), s32[]{:S(2)}) async-start(), calls=%async_computation.3 | async-start | bytes 2027520 | tf_op jit(solution)/shard_map/all_gather | solution.py:21
  7.9 308.3 %all-reduce.3.cloned.1.call-start = ((), (), s32[]{:S(2)}) async-start(), calls=%async_computation.4 | async-start | bytes 12582912 | tf_op jit(solution)/shard_map/psum | solution.py:27
  7.9 37.2 %copy-start.3 = (bf16[1280,2048]{1,0:T(8,128)(2,1)S(1)}, bf16[1280,2048]{1,0:T(8,128)(2,1)}, u32[]{:S(2)}) copy-start(bf16[1280,2048]{1,0:T(8,128)(2,1)} %param.8) | copy-start | bytes 15728644
  189.8 126.4 %copy-start.2 = (f32[2048]{0:T(1024)S(1)}, f32[2048]{0:T(1024)}, u32[]{:S(2)}) copy-start(f32[2048]{0:T(1024)} %param.9) | copy-start | bytes 24580
  189.8 299.9 %reduce-scatter.2.cloned.1.call-start = ((), (), s32[]{:S(2)}) async-start(), calls=%async_computation.2 | async-start | bytes 2027520 | tf_op jit(solution)/shard_map/reduce_scatter | solution.py:32
  316.2 9.1 %copy-start = (bf16[768,2048]{1,0:T(8,128)(2,1)S(1)}, bf16[768,2048]{1,0:T(8,128)(2,1)}, u32[]{:S(2)}) copy-start(bf16[768,2048]{1,0:T(8,128)(2,1)} %get-tuple-element.2) | copy-start | bytes 9437188
  325.4 164.3 %copy-start.1 = (f32[1280]{0:T(1024)S(1)}, f32[1280]{0:T(1024)}, u32[]{:S(2)}) copy-start(f32[1280]{0:T(1024)} %param.11) | copy-start | bytes 15364
Sparse Core Ops, SparseCore 0:
  9.6 171.1 all-gather.1
  190.0 126.2 all-reduce.2
  325.5 164.1 reduce-scatter.1

commit v2 on v0

--- a/solution.py
+++ b/solution.py
@@ -1,7 +1,15 @@
+import functools
 import jax
 import jax.numpy as jnp
 from jax import lax
 from jax.sharding import PartitionSpec as P
+
+
+def bring_gates(inner_x, net_axis):
+    return lax.all_gather(inner_x, net_axis).sum(axis=0)
+
+
+_render_entries = functools.partial(bring_gates, net_axis="narrow")
 
 
 def local(mlp_input, grad_rows, enc_weight, enc_bias, dec_weight, dec_bias):
@@ -17,7 +25,7 @@
         preferred_element_type=jnp.float32,
     )
     pre, grad_proj = (
-        lax.psum(enc_terms.astype(jnp.bfloat16), "narrow").astype(jnp.float32),
+        _render_entries(enc_terms.astype(jnp.bfloat16)).astype(jnp.float32),
         lax.psum(grad_terms.astype(jnp.bfloat16), "narrow").astype(jnp.float32),
     )
     latents = jnp.maximum(pre + enc_bias[None, :], 0.0).astype(jnp.bfloat16)

time: 637 us -> 659 us (1.035)
  waiting for transfers between devices: 589 us -> 603 us
  other arithmetic: 6.51 us -> 15.4 us
    all_gather x0 -> x1, waiting for transfers between devices: none -> 79.6 us  [bring_gates(): return lax.all_gather(inner_x, net_axis).sum(axis=0)]
    psum x1, waiting for transfers between devices: 127 us -> 59.8 us  [local(): lax.psum(grad_terms.astype(jnp.bfloat16), 'narrow').astype(jnp.float32)]
    all_gather x1, waiting for transfers between devices: 156 us -> 145 us  [local(): lax.all_gather(grad_rows, 'wide', axis=0, tiled=True)]
    all_gather x1, waiting for transfers between devices: 145 us -> 156 us  [local(): lax.all_gather(mlp_input, 'wide', axis=0, tiled=True)]
    reduce_sum x0 -> x1, other arithmetic: none -> 8.9 us  [bring_gates(): return lax.all_gather(inner_x, net_axis).sum(axis=0)]
  transfers between devices with their start and end apart: 4 -> 5, of which waited for: 4 -> 5; matrix products, arithmetic and copies ran while one was open for 2% -> 6% of each run, Pallas kernels for 0% -> 0%
where the time goes in v2:
time: 659 us
  waiting for transfers between devices  603 us (92%)
  matrix products  26.5 us (4%)
  other arithmetic  15.4 us (2%)
  between operations  13.8 us (2%)
    reduce_scatter x1, waiting for transfers between devices, local(): lax.psum_scatter(jnp.dot(latents, dec_weight, preferred_element_type=jnp....  161 us
    all_gather x1, waiting for transfers between devices, local(): lax.all_gather(mlp_input, 'wide', axis=0, tiled=True)  156 us
    all_gather x1, waiting for transfers between devices, local(): lax.all_gather(grad_rows, 'wide', axis=0, tiled=True)  145 us
    all_gather x1, waiting for transfers between devices, bring_gates(): return lax.all_gather(inner_x, net_axis).sum(axis=0)  79.6 us
    psum x1, waiting for transfers between devices, local(): lax.psum(grad_terms.astype(jnp.bfloat16), 'narrow').astype(jnp.float32)  59.8 us
  transfers between devices with their start and end apart: 5, of which 5 were waited for; matrix products, arithmetic and copies ran while one was open for 6% of the time, Pallas kernels for 0%

profile of v2, /device:TPU:0, one launch (start us, length us, event | category | flops | bytes accessed | tf_op | source)
XLA Modules:
  0.0 658.9 jit_solution(9086583643154458957)
XLA Ops:
  7.2 0.0 all-gather.5.cloned.1.call-start
  7.2 0.7 all-gather.5.cloned.1.call-update
  7.9 0.0 all-gather.7.cloned.1.call-start
  7.9 0.7 all-gather.7.cloned.1.call-update
  8.6 0.0 all-gather.9.cloned.1.call-start
  8.7 155.7 %all-gather.5.cloned.1.call-done = bf16[768,1280]{1,0:T(8,128)(2,1)} async-done(((bf16[24,1280]{1,0:T(8,128)(2,1)}), bf16[768,1280]{1,0:T(8,128)(2,1)}) %all-gather.5.cloned.1.call-update) | async-done | bytes 1966096 | tf_op jit(solution)/shard_map/all_gather | solution.py:17
  164.4 9.0 %convolution_convert_fusion.2 = bf16[768,2048]{1,0:T(8,128)(2,1)} fusion(bf16[768,1280]{1,0:T(8,128)(2,1)} %all-gather.5.cloned.1.call-done, bf16[1280,2048]{1,0:T(8,128)(2,1)} %param.8), kind=kOutput, calls=%fused_computation.4 | convolution fusion | flops 4028104704 | bytes 10354688 | tf_op jit(solution)/shard_map/dot_general | solution.py:16
  173.4 0.0 all-gather.9.cloned.1.call-update
  173.4 0.0 all-reduce.2.cloned.1.call-start
  173.4 145.1 %all-gather.7.cloned.1.call-done = bf16[768,1280]{1,0:T(8,128)(2,1)} async-done(((bf16[24,1280]{1,0:T(8,128)(2,1)}), bf16[768,1280]{1,0:T(8,128)(2,1)}) %all-gather.7.cloned.1.call-update) | async-done | bytes 1966096 | tf_op jit(solution)/shard_map/all_gather | solution.py:22
  318.5 9.0 %convolution_convert_fusion = bf16[768,2048]{1,0:T(8,128)(2,1)} fusion(bf16[768,1280]{1,0:T(8,128)(2,1)} %all-gather.7.cloned.1.call-done, bf16[2048,1280]{1,0:T(8,128)(2,1)} %param.10), kind=kOutput, calls=%fused_computation.2 | convolution fusion | flops 4028104704 | bytes 10354688 | tf_op jit(solution)/shard_map/dot_general | solution.py:21
  327.5 0.0 all-reduce.2.cloned.1.call-update
  327.5 0.2 reduce-scatter.2.cloned.1.call-start
  327.7 79.6 %all-gather.9.cloned.1.call-done = bf16[3072,2048]{1,0:T(8,128)(2,1)} async-done(((bf16[768,2048]{1,0:T(8,128)(2,1)}), bf16[3072,2048]{1,0:T(8,128)(2,1)}) %all-gather.9.cloned.1.call-update) | async-done | bytes 12582928 | tf_op jit(solution)/shard_map/all_gather | solution.py:9
  407.4 0.0 copy-start.1
  407.4 8.9 %reduce_sum.12 = bf16[768,2048]{1,0:T(8,128)(2,1)S(1)} reduce(bf16[4,768,2048]{2,1,0:T(8,128)(2,1)} %bitcast.6, bf16[]{:T(256)} %constant.1.clone.1), dimensions={0}, to_apply=%region_0.0 | reduce | flops 4718592 | bytes 15728642 | tf_op jit(solution)/shard_map/reduce_sum | solution.py:9
  416.3 0.0 copy-done.1
  416.3 8.5 %convolution_convert_fusion.1 = bf16[768,1280]{1,0:T(8,128)(2,1)} fusion(bf16[2048,1280]{1,0:T(8,128)(2,1)} %param.10, bf16[768,2048]{1,0:T(8,128)(2,1)S(1)} %reduce_sum.12, f32[2048]{0:T(1024)S(1)} %copy-done.1), kind=kOutput, calls=%fused_computation.3 | convolution fusion | flops 4033806336 | bytes 10362880 | tf_op jit(solution)/shard_map/dot_general | solution.py:34
  424.8 0.0 copy-start
  424.8 0.0 reduce-scatter.2.cloned.1.call-update
  424.8 59.8 %all-reduce.2.cloned.1.call-done = bf16[768,2048]{1,0:T(8,128)(2,1)} async-done(((bf16[768,2048]{1,0:T(8,128)(2,1)}), bf16[768,2048]{1,0:T(8,128)(2,1)}) %all-reduce.2.cloned.1.call-update) | async-done | bytes 3145744 | tf_op jit(solution)/shard_map/psum | solution.py:29
  484.6 5.0 multiply_convert_fusion
  489.6 161.2 %reduce-scatter.2.cloned.1.call-done = bf16[24,1280]{1,0:T(8,128)(2,1)} async-done(((bf16[768,1280]{1,0:T(8,128)(2,1)}), bf16[24,1280]{1,0:T(8,128)(2,1)}) %reduce-scatter.2.cloned.1.call-update) | async-done | bytes 61456 | tf_op jit(solution)/shard_map/reduce_scatter | solution.py:33
  650.9 0.0 copy-done
  650.9 1.5 add_convert_fusion
Async XLA Ops:
  7.2 157.2 %all-gather.5.cloned.1.call-start = ((), (), s32[]{:S(2)}) async-start(), calls=%async_computation.1 | async-start | bytes 2027520 | tf_op jit(solution)/shard_map/all_gather | solution.py:17
  7.9 310.6 %all-gather.7.cloned.1.call-start = ((), (), s32[]{:S(2)}) async-start(), calls=%async_computation.3 | async-start | bytes 2027520 | tf_op jit(solution)/shard_map/all_gather | solution.py:22
  8.6 398.7 %all-gather.9.cloned.1.call-start = ((), (), s32[]{:S(2)}) async-start(), calls=%async_computation.5 | async-start | bytes 15728640 | tf_op jit(solution)/shard_map/all_gather | solution.py:9
  173.4 311.3 %all-reduce.2.cloned.1.call-start = ((), (), s32[]{:S(2)}) async-start(), calls=%async_computation.4 | async-start | bytes 6291456 | tf_op jit(solution)/shard_map/psum | solution.py:29
  327.5 323.4 %reduce-scatter.2.cloned.1.call-start = ((), (), s32[]{:S(2)}) async-start(), calls=%async_computation.2 | async-start | bytes 2027520 | tf_op jit(solution)/shard_map/reduce_scatter | solution.py:33
  407.4 8.9 %copy-start.1 = (f32[2048]{0:T(1024)S(1)}, f32[2048]{0:T(1024)}, u32[]{:S(2)}) copy-start(f32[2048]{0:T(1024)} %param.9) | copy-start | bytes 24580
  424.8 226.1 %copy-start = (f32[1280]{0:T(1024)S(1)}, f32[1280]{0:T(1024)}, u32[]{:S(2)}) copy-start(f32[1280]{0:T(1024)} %param.11) | copy-start | bytes 15364
Sparse Core Ops, SparseCore 0:
  9.6 154.7 all-gather.4
  166.0 152.4 all-gather.6
  320.7 86.5 all-gather.8
  409.7 74.8 all-reduce.1
  486.9 163.9 reduce-scatter.1
